TPU v7x, 32 devices: a whole 2x2x4 slice. The times are simulated.
32 devices in a mesh: row: 8 (over y, x, core), col: 4 (over z).
Axes of the slice: x: 2, y: 2, z: 4, core: 2. Of those that a mesh axis runs over, the one named last changes fastest.
Arguments:
- panel: int32 [32], replicated, may hold values from 0 to 31, each once
- trailing: float32 [8192, 8192], P('row', 'col'), as said below
Outputs:
- factor_panels: float32 [8192, 768], P('row')
- schur: float32 [8192, 8192], P('row', 'col')
Inputs may be any that keep to these rules, and one draw needn't show every extreme that they name: panel names every block index once. In matrix order trailing is symmetric, and each diagonal block of 256 x 256 is strictly diagonally dominant with a positive diagonal.
All inputs are finite; a program needn't handle non-finite values.
Results may differ from a plain program's by a relative error of at most 0.0001.
Values sent between devices are 32-bit elements; how exact they have to be, the bound alone decides.
No kernel may reach another device: no remote copies, remote signals or barrier semaphores. Data moves between devices by JAX's collectives and lax.ppermute only.
A program may use at most 128 MiB of HBM per device.

v0:
```python
import jax
import jax.numpy as jnp
from jax import lax
from jax.sharding import PartitionSpec as P

NB = 256
PANELS = 3


def spread(value, axis, source):
    kept = jnp.where(lax.axis_index(axis) == source, value, 0).astype(value.dtype)
    return lax.psum(kept, axis)


def solve_panel(columns, corner):
    lower = jnp.linalg.cholesky(corner)
    identity = jnp.eye(corner.shape[0], dtype=jnp.float32)
    inverse = lax.linalg.triangular_solve(lower, identity, left_side=True, lower=True)
    return jnp.dot(
        columns, inverse.T, precision=lax.Precision.HIGHEST, preferred_element_type=jnp.float32
    )


def on_device(panel, trailing):
    rows_all = lax.axis_size("row")
    cols_all = lax.axis_size("col")
    my_row = lax.axis_index("row")
    my_col = lax.axis_index("col")
    loc_rows, loc_cols = trailing.shape
    blk_rows = loc_rows // NB
    blk_cols = loc_cols // NB
    ratio = rows_all // cols_all
    row_ids = jnp.arange(loc_rows, dtype=jnp.int32) // NB
    col_ids = jnp.arange(loc_cols, dtype=jnp.int32) // NB
    current = trailing
    factors = []
    for step in range(PANELS):
        pivot = panel[step]
        owner_row = pivot % rows_all
        local_row = pivot // rows_all
        owner_col = pivot % cols_all
        local_col = pivot // cols_all
        columns = lax.dynamic_slice_in_dim(current, local_col * NB, NB, 1)
        corner = lax.dynamic_slice_in_dim(columns, local_row * NB, NB, 0)
        pivot_tile = spread(corner, "row", owner_row)
        row_factor = spread(solve_panel(columns, pivot_tile), "col", owner_col)
        pieces = []
        for offset in range(ratio):
            fetched = spread(row_factor, "row", my_col + offset * cols_all)
            pieces.append(fetched.reshape(blk_rows, NB, NB))
        col_factor = jnp.stack(pieces, axis=1).reshape(blk_cols * NB, NB)
        update = lax.dot_general(
            row_factor,
            col_factor,
            (((1,), (1,)), ((), ())),
            precision=lax.Precision.HIGHEST,
            preferred_element_type=jnp.float32,
        )
        current = current - update
        keep_rows = (row_ids != local_row) | (my_row != owner_row)
        keep_cols = (col_ids != local_col) | (my_col != owner_col)
        current = jnp.where(keep_rows[:, None] & keep_cols[None, :], current, jnp.float32(0.0))
        factors.append(row_factor)
    return (jnp.concatenate(factors, axis=1), current)


def solution(mesh):
    in_specs = (P(), P("row", "col"))
    out_specs = (P("row", None), P("row", "col"))
    return jax.shard_map(
        on_device, mesh=mesh, in_specs=in_specs, out_specs=out_specs, check_vma=False
    )
```

profile of v0, /device:TPU:0, one launch (start us, length us, event | category | flops | bytes accessed | tf_op | source)
XLA Modules:
  0.0 797.8 jit_solution(4477696324197038148)
XLA Ops:
  7.2 1.4 fusion.64
  11.3 9.3 %copy.13 = f32[1024,2048]{0,1:T(8,128)} copy(f32[1024,2048]{1,0:T(8,128)} %param.6) | data formatting | bytes 16777216 | tf_op args[1]
  20.5 1.8 dynamic-slice_select_fusion.2
  22.5 56.7 %all-reduce.14.cloned.1.call-done = f32[256,256]{0,1:T(8,128)} async-done(((f32[256,256]{0,1:T(8,128)}), f32[256,256]{0,1:T(8,128)}) %all-reduce.14.cloned.1.call-update) | async-done | bytes 262160 | tf_op jit(solution)/shard_map/psum | solution.py:12
  81.2 11.7 %cholesky.172 = f32[128,128]{1,0:T(8,128)S(1)} custom-call(f32[128,128]{1,0:T(8,128)S(1)} %cholesky.270), custom_call_target="Cholesky" | custom-call | tf_op jit(solution)/shard_map/jit(cholesky)/cholesky | solution.py:16
  93.0 9.8 %custom-call.15 = f32[1,128,128]{1,2,0:T(8,128)S(1)} custom-call(f32[1,128,128]{2,1,0:T(8,128)S(1)} %get-tuple-element.84), custom_call_target="InvertDiagBlocksLowerTriangular" | custom-call | tf_op jit(solution)/shard_map/jit(cholesky)/cholesky | solution.py:16
  103.3 11.7 %cholesky.189 = f32[128,128]{1,0:T(8,128)S(1)} custom-call(f32[128,128]{1,0:T(8,128)S(1)} %convolution_subtract_fusion.5), custom_call_target="Cholesky" | custom-call | tf_op jit(solution)/shard_map/jit(cholesky)/cholesky | solution.py:16
  117.2 4.3 while.6
  120.1 1.4 bitcast_dynamic-update-slice_fusion.6
  121.5 19.7 %custom-call.16 = f32[2,128,128]{1,2,0:T(8,128)S(1)} custom-call(f32[2,128,128]{2,1,0:T(8,128)S(1)} %get-tuple-element.24), custom_call_target="InvertDiagBlocksLowerTriangular" | custom-call | tf_op jit(solution)/shard_map/triangular_solve/custom-call.0 | solution.py:18
  142.1 3.2 convolution_select_fusion.2
  145.4 51.4 %all-reduce.16.cloned.1.call-done = f32[1024,256]{1,0:T(8,128)} async-done(((f32[1024,256]{1,0:T(8,128)}), f32[1024,256]{1,0:T(8,128)}) %all-reduce.16.cloned.1.call-update) | async-done | bytes 1048592 | tf_op jit(solution)/shard_map/psum | solution.py:12
  196.8 2.7 broadcast_select_fusion.5
  202.5 59.3 %all-reduce.30.cloned.1.call-done = (f32[4,1,256,256]{3,2,1,0:T(8,128)}, f32[4,1,256,256]{3,2,1,0:T(8,128)}) async-done(((f32[4,1,256,256]{3,2,1,0:T(8,128)}, f32[4,1,256,256]{3,2,1,0:T(8,128)}), (f32[4,1,256,256]{3,2,1,0:T(8,128)}, f32[4,1,256,256]{3,2,1,0:T(8,128)})) %all-reduce.30.cloned.1.call-update) | async-done | bytes 2097168 | tf_op jit(solution)/shard_map/psum | solution.py:12
  261.8 1.8 pad_maximum_fusion.1
  263.6 10.4 %subtract_select_fusion.2 = f32[1024,2048]{0,1:T(8,128)S(1)} fusion(f32[1024,2048]{0,1:T(8,128)} %copy.13, f32[1024,256]{1,0:T(8,128)S(1)} %copy-done.2, f32[2048,256]{1,0:T(8,128)S(1)} %bitcast.124, pred[1024]{0:T(1024)(128)(4,1)S(1)} %fusion.51, pred[2048]{0:T(1024)(128)(4,1)S(1)} %fusion.42), kind=kOutput, calls=%fused_computation.8 | convolution fusion | flops 6448742400 | bytes 19926016 | tf_op jit(solution)/shard_map/dot_general | solution.py:52
  274.0 3.4 copy-done
  278.7 52.6 %all-reduce.18.cloned.1.call-done = f32[256,256]{0,1:T(8,128)} async-done(((f32[256,256]{0,1:T(8,128)}), f32[256,256]{0,1:T(8,128)}) %all-reduce.18.cloned.1.call-update) | async-done | bytes 262160 | tf_op jit(solution)/shard_map/psum | solution.py:12
  333.4 11.7 %cholesky.206 = f32[128,128]{1,0:T(8,128)S(1)} custom-call(f32[128,128]{1,0:T(8,128)S(1)} %cholesky.273), custom_call_target="Cholesky" | custom-call | tf_op jit(solution)/shard_map/jit(cholesky)/cholesky | solution.py:16
  345.8 9.8 %custom-call.17 = f32[1,128,128]{1,2,0:T(8,128)S(1)} custom-call(f32[1,128,128]{2,1,0:T(8,128)S(1)} %get-tuple-element.80), custom_call_target="InvertDiagBlocksLowerTriangular" | custom-call | tf_op jit(solution)/shard_map/jit(cholesky)/cholesky | solution.py:16
  356.1 11.7 %cholesky.223 = f32[128,128]{1,0:T(8,128)S(1)} custom-call(f32[128,128]{1,0:T(8,128)S(1)} %convolution_subtract_fusion.4), custom_call_target="Cholesky" | custom-call | tf_op jit(solution)/shard_map/jit(cholesky)/cholesky | solution.py:16
  370.0 4.3 while.7
  370.8 1.4 bitcast_dynamic-update-slice_fusion.7
  372.9 1.4 bitcast_dynamic-update-slice_fusion.7
  374.3 19.7 %custom-call.18 = f32[2,128,128]{1,2,0:T(8,128)S(1)} custom-call(f32[2,128,128]{2,1,0:T(8,128)S(1)} %get-tuple-element.25), custom_call_target="InvertDiagBlocksLowerTriangular" | custom-call | tf_op jit(solution)/shard_map/triangular_solve/custom-call.0 | solution.py:18
  394.9 4.0 convolution_select_fusion.1
  399.0 51.4 %all-reduce.20.cloned.1.call-done = f32[1024,256]{1,0:T(8,128)} async-done(((f32[1024,256]{1,0:T(8,128)}), f32[1024,256]{1,0:T(8,128)}) %all-reduce.20.cloned.1.call-update) | async-done | bytes 1048592 | tf_op jit(solution)/shard_map/psum | solution.py:12
  450.4 2.7 broadcast_select_fusion.3
  455.7 59.5 %all-reduce.28.cloned.1.call-done = (f32[4,1,256,256]{3,2,1,0:T(8,128)}, f32[4,1,256,256]{3,2,1,0:T(8,128)}) async-done(((f32[4,1,256,256]{3,2,1,0:T(8,128)}, f32[4,1,256,256]{3,2,1,0:T(8,128)}), (f32[4,1,256,256]{3,2,1,0:T(8,128)}, f32[4,1,256,256]{3,2,1,0:T(8,128)})) %all-reduce.28.cloned.1.call-update) | async-done | bytes 2097168 | tf_op jit(solution)/shard_map/psum | solution.py:12
  515.2 1.8 pad_maximum_fusion.2
  517.0 10.4 %subtract_select_fusion.1 = f32[1024,2048]{0,1:T(8,128)S(1)} fusion(f32[1024,2048]{0,1:T(8,128)} %copy-done, f32[1024,256]{1,0:T(8,128)S(1)} %copy-done.3, f32[2048,256]{1,0:T(8,128)S(1)} %bitcast.125, pred[1024]{0:T(1024)(128)(4,1)S(1)} %fusion.52, pred[2048]{0:T(1024)(128)(4,1)S(1)} %fusion.43), kind=kOutput, calls=%fused_computation.7 | convolution fusion | flops 6448742400 | bytes 19926016 | tf_op jit(solution)/shard_map/dot_general | solution.py:52
  527.4 3.4 copy-done.1
  531.9 52.8 %all-reduce.22.cloned.1.call-done = f32[256,256]{0,1:T(8,128)} async-done(((f32[256,256]{0,1:T(8,128)}), f32[256,256]{0,1:T(8,128)}) %all-reduce.22.cloned.1.call-update) | async-done | bytes 262160 | tf_op jit(solution)/shard_map/psum | solution.py:12
  586.8 11.7 %cholesky.240 = f32[128,128]{1,0:T(8,128)S(1)} custom-call(f32[128,128]{1,0:T(8,128)S(1)} %cholesky.276), custom_call_target="Cholesky" | custom-call | tf_op jit(solution)/shard_map/jit(cholesky)/cholesky | solution.py:16
  599.2 9.8 %custom-call.19 = f32[1,128,128]{1,2,0:T(8,128)S(1)} custom-call(f32[1,128,128]{2,1,0:T(8,128)S(1)} %get-tuple-element.76), custom_call_target="InvertDiagBlocksLowerTriangular" | custom-call | tf_op jit(solution)/shard_map/jit(cholesky)/cholesky | solution.py:16
  609.5 11.7 %cholesky.257 = f32[128,128]{1,0:T(8,128)S(1)} custom-call(f32[128,128]{1,0:T(8,128)S(1)} %convolution_subtract_fusion.3), custom_call_target="Cholesky" | custom-call | tf_op jit(solution)/shard_map/jit(cholesky)/cholesky | solution.py:16
  623.4 4.4 while.8
  624.3 1.4 bitcast_dynamic-update-slice_fusion.8
  626.3 1.4 bitcast_dynamic-update-slice_fusion.8
  627.7 19.7 %custom-call.20 = f32[2,128,128]{1,2,0:T(8,128)S(1)} custom-call(f32[2,128,128]{2,1,0:T(8,128)S(1)} %get-tuple-element.26), custom_call_target="InvertDiagBlocksLowerTriangular" | custom-call | tf_op jit(solution)/shard_map/triangular_solve/custom-call.0 | solution.py:18
  648.3 4.0 convolution_select_fusion
  652.4 51.4 %all-reduce.24.cloned.1.call-done = f32[1024,256]{1,0:T(8,128)} async-done(((f32[1024,256]{1,0:T(8,128)}), f32[1024,256]{1,0:T(8,128)}) %all-reduce.24.cloned.1.call-update) | async-done | bytes 1048592 | tf_op jit(solution)/shard_map/psum | solution.py:12
  703.8 2.8 broadcast_select_fusion.1
  706.7 1.9 pad_maximum_fusion
  708.6 59.7 %all-reduce.26.cloned.1.call-done = (f32[4,1,256,256]{3,2,1,0:T(8,128)}, f32[4,1,256,256]{3,2,1,0:T(8,128)}) async-done(((f32[4,1,256,256]{3,2,1,0:T(8,128)}, f32[4,1,256,256]{3,2,1,0:T(8,128)}), (f32[4,1,256,256]{3,2,1,0:T(8,128)}, f32[4,1,256,256]{3,2,1,0:T(8,128)})) %all-reduce.26.cloned.1.call-update) | async-done | bytes 2097168 | tf_op jit(solution)/shard_map/psum | solution.py:12
  768.3 1.8 pad_maximum_fusion.3
  770.1 11.7 %subtract_select_fusion = f32[1024,2048]{0,1:T(8,128)} fusion(f32[1024,2048]{0,1:T(8,128)} %copy-done.1, f32[1024,256]{1,0:T(8,128)S(1)} %copy-done.4, f32[2048,256]{1,0:T(8,128)S(1)} %bitcast.123, pred[1024]{0:T(1024)(128)(4,1)S(1)} %fusion.53, pred[2048]{0:T(1024)(128)(4,1)S(1)} %fusion.44), kind=kOutput, calls=%fused_computation.6 | convolution fusion | flops 6448742400 | bytes 19926016 | tf_op jit(solution)/shard_map/dot_general | solution.py:52
  781.8 9.1 %copy.27 = f32[1024,2048]{1,0:T(8,128)} copy(f32[1024,2048]{0,1:T(8,128)} %subtract_select_fusion) | data formatting | bytes 16777216
  (94 shorter events, 22.1 us)
Async XLA Ops:
  7.2 72.0 %all-reduce.14.cloned.1.call-start = ((), (), s32[]{:S(2)}) async-start(), calls=%async_computation | async-start | bytes 524288 | tf_op jit(solution)/shard_map/psum | solution.py:12
  22.4 174.5 %all-reduce.16.cloned.1.call-start = ((), (), s32[]{:S(2)}) async-start(), calls=%async_computation.1 | async-start | bytes 2097152 | tf_op jit(solution)/shard_map/psum | solution.py:12
  145.4 116.5 %all-reduce.30.cloned.1.call-start = ((), (), s32[]{:S(2)}) async-start(), calls=%async_computation.8 | async-start | bytes 4194304 | tf_op jit(solution)/shard_map/psum | solution.py:12
  199.5 64.1 %copy-start.2 = (f32[1024,256]{1,0:T(8,128)S(1)}, f32[1024,256]{1,0:T(8,128)}, u32[]{:S(2)}) copy-start(f32[1024,256]{1,0:T(8,128)} %all-reduce.16.cloned.1.call-done) | copy-start | bytes 3145732
  199.5 131.8 %all-reduce.18.cloned.1.call-start = ((), (), s32[]{:S(2)}) async-start(), calls=%async_computation.2 | async-start | bytes 524288 | tf_op jit(solution)/shard_map/psum | solution.py:12
  274.0 3.4 copy-start
  278.3 172.1 %all-reduce.20.cloned.1.call-start = ((), (), s32[]{:S(2)}) async-start(), calls=%async_computation.3 | async-start | bytes 2097152 | tf_op jit(solution)/shard_map/psum | solution.py:12
  398.9 116.3 %all-reduce.28.cloned.1.call-start = ((), (), s32[]{:S(2)}) async-start(), calls=%async_computation.7 | async-start | bytes 4194304 | tf_op jit(solution)/shard_map/psum | solution.py:12
  453.1 63.9 %copy-start.3 = (f32[1024,256]{1,0:T(8,128)S(1)}, f32[1024,256]{1,0:T(8,128)}, u32[]{:S(2)}) copy-start(f32[1024,256]{1,0:T(8,128)} %all-reduce.20.cloned.1.call-done) | copy-start | bytes 3145732
  453.1 131.6 %all-reduce.22.cloned.1.call-start = ((), (), s32[]{:S(2)}) async-start(), calls=%async_computation.4 | async-start | bytes 524288 | tf_op jit(solution)/shard_map/psum | solution.py:12
  527.4 3.4 copy-start.1
  531.6 172.2 %all-reduce.24.cloned.1.call-start = ((), (), s32[]{:S(2)}) async-start(), calls=%async_computation.5 | async-start | bytes 2097152 | tf_op jit(solution)/shard_map/psum | solution.py:12
  652.4 115.9 %all-reduce.26.cloned.1.call-start = ((), (), s32[]{:S(2)}) async-start(), calls=%async_computation.6 | async-start | bytes 4194304 | tf_op jit(solution)/shard_map/psum | solution.py:12
  703.8 2.9 copy-start.4
Sparse Core Ops, SparseCore 0:
  22.5 56.5 all-reduce.13
  145.5 51.2 all-reduce.15
  200.7 61.1 all-reduce.29
  278.4 52.9 all-reduce.17
  399.0 51.2 all-reduce.19
  454.1 61.1 all-reduce.27
  531.8 52.9 all-reduce.21
  652.5 51.2 all-reduce.23
  707.1 61.1 all-reduce.25
where the time goes:
time: 807 us; the launch traced here: 798 us
  waiting for transfers between devices  495 us (61%)
  other arithmetic  184 us (23%)
  matrix products  47.7 us (6%)
  local copies, waits for them, and re-layouts  42.2 us (5%)
  between operations  26.9 us (3%)
    psum x9, waiting for transfers between devices, spread(): return lax.psum(kept, axis)  495 us
    another operation x20, other arithmetic, solve_panel(): lower = jnp.linalg.cholesky(corner)  103 us
    another operation x7, other arithmetic, solve_panel(): lax.linalg.triangular_solve(lower, identity, left_side=True, lower=True)  59.1 us
    dot_general x3, matrix products, on_device(): lax.dot_general(row_factor, col_factor, (((1,), (1,)), ((), ())), precisi...  32.4 us
    unnamed x12, local copies, waits for them, and re-layouts  25.2 us
  transfers between devices with their start and end apart: 9, of which 9 were waited for; matrix products, arithmetic and copies ran while one was open for 0% of the time, Pallas kernels for 0%

commit v1 on v0

--- a/solution.py
+++ b/solution.py
@@ -7,9 +7,13 @@
 PANELS = 3
 
 
+def _arrange_array(tile_in, a_name):
+    return jnp.sum(lax.all_gather(tile_in, a_name), axis=0)
+
+
 def spread(value, axis, source):
     kept = jnp.where(lax.axis_index(axis) == source, value, 0).astype(value.dtype)
-    return lax.psum(kept, axis)
+    return _arrange_array(kept, axis)
 
 
 def solve_panel(columns, corner):

time: 807 us -> 954 us (1.18)
  waiting for transfers between devices: 495 us -> 636 us
  other arithmetic: 184 us -> 213 us
  local copies, waits for them, and re-layouts: 42.2 us -> 20.9 us
    all_gather x0 -> x12, waiting for transfers between devices: none -> 634 us  [_arrange_array(): return jnp.sum(lax.all_gather(tile_in, a_name), axis=0)]
    psum x9 -> x0, waiting for transfers between devices: 495 us -> none  [spread(): return lax.psum(kept, axis)]
    reduce_sum x0 -> x12, other arithmetic: none -> 38.4 us  [_arrange_array(): return jnp.sum(lax.all_gather(tile_in, a_name), axis=0)]
    unnamed x12 -> x4, local copies, waits for them, and re-layouts: 25.2 us -> 6.78 us
  transfers between devices with their start and end apart: 9 -> 12, of which waited for: 9 -> 12; matrix products, arithmetic and copies ran while one was open for 0% -> 1% of each run, Pallas kernels for 0% -> 0%
where the time goes in v1:
time: 954 us; the launch traced here: 945 us
  waiting for transfers between devices  636 us (67%)
  other arithmetic  213 us (22%)
  matrix products  46.2 us (5%)
  between operations  27 us (3%)
  local copies, waits for them, and re-layouts  20.9 us (2%)
    all_gather x12, waiting for transfers between devices, _arrange_array(): return jnp.sum(lax.all_gather(tile_in, a_name), axis=0)  634 us
    another operation x20, other arithmetic, solve_panel(): lower = jnp.linalg.cholesky(corner)  103 us
    another operation x7, other arithmetic, solve_panel(): lax.linalg.triangular_solve(lower, identity, left_side=True, lower=True)  59.1 us
    reduce_sum x12, other arithmetic, _arrange_array(): return jnp.sum(lax.all_gather(tile_in, a_name), axis=0)  38.4 us
    dot_general x3, matrix products, on_device(): lax.dot_general(row_factor, col_factor, (((1,), (1,)), ((), ())), precisi...  32.5 us
  transfers between devices with their start and end apart: 12, of which 12 were waited for; matrix products, arithmetic and copies ran while one was open for 1% of the time, Pallas kernels for 0%

profile of v1, /device:TPU:0, one launch (start us, length us, event | category | flops | bytes accessed | tf_op | source)
XLA Modules:
  0.0 944.9 jit_solution(6562544745476999213)
XLA Ops:
  11.3 1.9 dynamic-slice_select_fusion.2
  13.3 30.6 %all-gather.25.cloned.1.call-done = f32[2048,256]{1,0:T(8,128)} async-done(((f32[256,256]{1,0:T(8,128)}), f32[2048,256]{1,0:T(8,128)}) %all-gather.25.cloned.1.call-update) | async-done | bytes 2097168 | tf_op jit(solution)/shard_map/all_gather | solution.py:11
  43.8 1.8 reduce_sum.108
  45.8 11.7 %cholesky.172 = f32[128,128]{1,0:T(8,128)S(1)} custom-call(f32[128,128]{1,0:T(8,128)S(1)} %cholesky.270), custom_call_target="Cholesky" | custom-call | tf_op jit(solution)/shard_map/jit(cholesky)/cholesky | solution.py:20
  57.5 9.8 %custom-call.15 = f32[1,128,128]{1,2,0:T(8,128)S(1)} custom-call(f32[1,128,128]{2,1,0:T(8,128)S(1)} %get-tuple-element.74), custom_call_target="InvertDiagBlocksLowerTriangular" | custom-call | tf_op jit(solution)/shard_map/jit(cholesky)/cholesky | solution.py:20
  67.8 11.7 %cholesky.189 = f32[128,128]{1,0:T(8,128)S(1)} custom-call(f32[128,128]{1,0:T(8,128)S(1)} %convolution_subtract_fusion.5), custom_call_target="Cholesky" | custom-call | tf_op jit(solution)/shard_map/jit(cholesky)/cholesky | solution.py:20
  81.8 4.3 while.6
  86.1 19.7 %custom-call.16 = f32[2,128,128]{1,2,0:T(8,128)S(1)} custom-call(f32[2,128,128]{2,1,0:T(8,128)S(1)} %get-tuple-element.24), custom_call_target="InvertDiagBlocksLowerTriangular" | custom-call | tf_op jit(solution)/shard_map/triangular_solve/custom-call.0 | solution.py:22
  106.7 3.2 convolution_select_fusion.2
  110.0 80.8 %all-gather.27.cloned.1.call-done = f32[4096,256]{1,0:T(8,128)} async-done(((f32[1024,256]{1,0:T(8,128)}), f32[4096,256]{1,0:T(8,128)}) %all-gather.27.cloned.1.call-update) | async-done | bytes 4194320 | tf_op jit(solution)/shard_map/all_gather | solution.py:11
  190.8 2.6 reduce_sum.109
  197.9 49.9 %all-gather.29.cloned.1.call-done = f32[8192,256]{1,0:T(8,128)} async-done(((f32[1024,256]{1,0:T(8,128)}), f32[8192,256]{1,0:T(8,128)}) %all-gather.29.cloned.1.call-update) | async-done | bytes 8388624 | tf_op jit(solution)/shard_map/all_gather | solution.py:11
  247.8 4.1 reduce_sum.110
  251.9 52.5 %all-gather.31.cloned.1.call-done = f32[8192,256]{1,0:T(8,128)} async-done(((f32[1024,256]{1,0:T(8,128)}), f32[8192,256]{1,0:T(8,128)}) %all-gather.31.cloned.1.call-update) | async-done | bytes 8388624 | tf_op jit(solution)/shard_map/all_gather | solution.py:11
  304.4 4.1 reduce_sum.111
  308.7 10.4 %subtract_select_fusion.2 = f32[1024,2048]{1,0:T(8,128)S(1)} fusion(f32[1024,2048]{1,0:T(8,128)} %param.6, f32[1024,256]{1,0:T(8,128)S(1)} %reduce_sum.109, f32[2048,256]{1,0:T(8,128)S(1)} %bitcast.131, pred[2048]{0:T(1024)(128)(4,1)S(1)} %fusion.42, pred[1024]{0:T(1024)(128)(4,1)S(1)} %fusion.51), kind=kOutput, calls=%fused_computation.8 | convolution fusion | flops 6448742400 | bytes 19926016 | tf_op jit(solution)/shard_map/dot_general | solution.py:56
  319.1 3.4 copy-done
  323.8 27.5 %all-gather.33.cloned.1.call-done = f32[2048,256]{1,0:T(8,128)} async-done(((f32[256,256]{1,0:T(8,128)}), f32[2048,256]{1,0:T(8,128)}) %all-gather.33.cloned.1.call-update) | async-done | bytes 2097168 | tf_op jit(solution)/shard_map/all_gather | solution.py:11
  351.3 1.8 reduce_sum.112
  353.3 11.7 %cholesky.206 = f32[128,128]{1,0:T(8,128)S(1)} custom-call(f32[128,128]{1,0:T(8,128)S(1)} %cholesky.273), custom_call_target="Cholesky" | custom-call | tf_op jit(solution)/shard_map/jit(cholesky)/cholesky | solution.py:20
  365.0 9.8 %custom-call.17 = f32[1,128,128]{1,2,0:T(8,128)S(1)} custom-call(f32[1,128,128]{2,1,0:T(8,128)S(1)} %get-tuple-element.70), custom_call_target="InvertDiagBlocksLowerTriangular" | custom-call | tf_op jit(solution)/shard_map/jit(cholesky)/cholesky | solution.py:20
  375.3 11.7 %cholesky.223 = f32[128,128]{1,0:T(8,128)S(1)} custom-call(f32[128,128]{1,0:T(8,128)S(1)} %convolution_subtract_fusion.4), custom_call_target="Cholesky" | custom-call | tf_op jit(solution)/shard_map/jit(cholesky)/cholesky | solution.py:20
  389.8 4.3 while.7
  394.1 19.7 %custom-call.18 = f32[2,128,128]{1,2,0:T(8,128)S(1)} custom-call(f32[2,128,128]{2,1,0:T(8,128)S(1)} %get-tuple-element.25), custom_call_target="InvertDiagBlocksLowerTriangular" | custom-call | tf_op jit(solution)/shard_map/triangular_solve/custom-call.0 | solution.py:22
  414.7 3.2 convolution_select_fusion.1
  418.0 80.8 %all-gather.35.cloned.1.call-done = f32[4096,256]{1,0:T(8,128)} async-done(((f32[1024,256]{1,0:T(8,128)}), f32[4096,256]{1,0:T(8,128)}) %all-gather.35.cloned.1.call-update) | async-done | bytes 4194320 | tf_op jit(solution)/shard_map/all_gather | solution.py:11
  498.8 2.6 reduce_sum.113
  506.6 49.3 %all-gather.37.cloned.1.call-done = f32[8192,256]{1,0:T(8,128)} async-done(((f32[1024,256]{1,0:T(8,128)}), f32[8192,256]{1,0:T(8,128)}) %all-gather.37.cloned.1.call-update) | async-done | bytes 8388624 | tf_op jit(solution)/shard_map/all_gather | solution.py:11
  555.8 4.1 reduce_sum.114
  559.9 52.1 %all-gather.39.cloned.1.call-done = f32[8192,256]{1,0:T(8,128)} async-done(((f32[1024,256]{1,0:T(8,128)}), f32[8192,256]{1,0:T(8,128)}) %all-gather.39.cloned.1.call-update) | async-done | bytes 8388624 | tf_op jit(solution)/shard_map/all_gather | solution.py:11
  612.0 5.0 reduce_sum.115
  618.5 10.4 %subtract_select_fusion.1 = f32[1024,2048]{1,0:T(8,128)S(1)} fusion(f32[1024,2048]{1,0:T(8,128)} %copy-done, f32[1024,256]{1,0:T(8,128)S(1)} %reduce_sum.113, f32[2048,256]{1,0:T(8,128)S(1)} %bitcast.130, pred[2048]{0:T(1024)(128)(4,1)S(1)} %fusion.43, pred[1024]{0:T(1024)(128)(4,1)S(1)} %fusion.52), kind=kOutput, calls=%fused_computation.7 | convolution fusion | flops 6448742400 | bytes 19926016 | tf_op jit(solution)/shard_map/dot_general | solution.py:56
  628.9 3.4 copy-done.1
  633.4 27.6 %all-gather.41.cloned.1.call-done = f32[2048,256]{1,0:T(8,128)} async-done(((f32[256,256]{1,0:T(8,128)}), f32[2048,256]{1,0:T(8,128)}) %all-gather.41.cloned.1.call-update) | async-done | bytes 2097168 | tf_op jit(solution)/shard_map/all_gather | solution.py:11
  663.0 11.7 %cholesky.240 = f32[128,128]{1,0:T(8,128)S(1)} custom-call(f32[128,128]{1,0:T(8,128)S(1)} %cholesky.276), custom_call_target="Cholesky" | custom-call | tf_op jit(solution)/shard_map/jit(cholesky)/cholesky | solution.py:20
  674.8 9.8 %custom-call.19 = f32[1,128,128]{1,2,0:T(8,128)S(1)} custom-call(f32[1,128,128]{2,1,0:T(8,128)S(1)} %get-tuple-element.66), custom_call_target="InvertDiagBlocksLowerTriangular" | custom-call | tf_op jit(solution)/shard_map/jit(cholesky)/cholesky | solution.py:20
  685.1 11.7 %cholesky.257 = f32[128,128]{1,0:T(8,128)S(1)} custom-call(f32[128,128]{1,0:T(8,128)S(1)} %convolution_subtract_fusion.3), custom_call_target="Cholesky" | custom-call | tf_op jit(solution)/shard_map/jit(cholesky)/cholesky | solution.py:20
  699.6 4.4 while.8
  704.0 19.7 %custom-call.20 = f32[2,128,128]{1,2,0:T(8,128)S(1)} custom-call(f32[2,128,128]{2,1,0:T(8,128)S(1)} %get-tuple-element.26), custom_call_target="InvertDiagBlocksLowerTriangular" | custom-call | tf_op jit(solution)/shard_map/triangular_solve/custom-call.0 | solution.py:22
  724.6 3.2 convolution_select_fusion
  727.9 80.8 %all-gather.43.cloned.1.call-done = f32[4096,256]{1,0:T(8,128)} async-done(((f32[1024,256]{1,0:T(8,128)}), f32[4096,256]{1,0:T(8,128)}) %all-gather.43.cloned.1.call-update) | async-done | bytes 4194320 | tf_op jit(solution)/shard_map/all_gather | solution.py:11
  808.7 2.6 reduce_sum.117
  813.4 1.9 pad_maximum_fusion
  815.3 50.4 %all-gather.45.cloned.1.call-done = f32[8192,256]{1,0:T(8,128)} async-done(((f32[1024,256]{1,0:T(8,128)}), f32[8192,256]{1,0:T(8,128)}) %all-gather.45.cloned.1.call-update) | async-done | bytes 8388624 | tf_op jit(solution)/shard_map/all_gather | solution.py:11
  865.7 4.1 reduce_sum.118
  869.8 52.0 %all-gather.47.cloned.1.call-done = f32[8192,256]{1,0:T(8,128)} async-done(((f32[1024,256]{1,0:T(8,128)}), f32[8192,256]{1,0:T(8,128)}) %all-gather.47.cloned.1.call-update) | async-done | bytes 8388624 | tf_op jit(solution)/shard_map/all_gather | solution.py:11
  921.8 4.1 reduce_sum.119
  926.0 11.6 %subtract_select_fusion = f32[1024,2048]{1,0:T(8,128)} fusion(f32[1024,2048]{1,0:T(8,128)} %copy-done.1, f32[1024,256]{1,0:T(8,128)S(1)} %reduce_sum.117, f32[2048,256]{1,0:T(8,128)S(1)} %bitcast.129, pred[2048]{0:T(1024)(128)(4,1)S(1)} %fusion.44, pred[1024]{0:T(1024)(128)(4,1)S(1)} %fusion.53), kind=kOutput, calls=%fused_computation.6 | convolution fusion | flops 6448742400 | bytes 19926016 | tf_op jit(solution)/shard_map/dot_general | solution.py:56
  (107 shorter events, 34.8 us)
Async XLA Ops:
  7.2 36.7 %all-gather.25.cloned.1.call-start = ((), (), s32[]{:S(2)}) async-start(), calls=%async_computation | async-start | bytes 2359296 | tf_op jit(solution)/shard_map/all_gather | solution.py:11
  13.2 177.7 %all-gather.27.cloned.1.call-start = ((), (), s32[]{:S(2)}) async-start(), calls=%async_computation.1 | async-start | bytes 5242880 | tf_op jit(solution)/shard_map/all_gather | solution.py:11
  109.9 137.9 %all-gather.29.cloned.1.call-start = ((), (), s32[]{:S(2)}) async-start(), calls=%async_computation.2 | async-start | bytes 9437184 | tf_op jit(solution)/shard_map/all_gather | solution.py:11
  194.9 109.5 %all-gather.31.cloned.1.call-start = ((), (), s32[]{:S(2)}) async-start(), calls=%async_computation.3 | async-start | bytes 9437184 | tf_op jit(solution)/shard_map/all_gather | solution.py:11
  195.5 155.8 %all-gather.33.cloned.1.call-start = ((), (), s32[]{:S(2)}) async-start(), calls=%async_computation.4 | async-start | bytes 2359296 | tf_op jit(solution)/shard_map/all_gather | solution.py:11
  319.1 3.4 copy-start
  323.4 175.5 %all-gather.35.cloned.1.call-start = ((), (), s32[]{:S(2)}) async-start(), calls=%async_computation.5 | async-start | bytes 5242880 | tf_op jit(solution)/shard_map/all_gather | solution.py:11
  417.9 137.9 %all-gather.37.cloned.1.call-start = ((), (), s32[]{:S(2)}) async-start(), calls=%async_computation.6 | async-start | bytes 9437184 | tf_op jit(solution)/shard_map/all_gather | solution.py:11
  502.9 109.1 %all-gather.39.cloned.1.call-start = ((), (), s32[]{:S(2)}) async-start(), calls=%async_computation.7 | async-start | bytes 9437184 | tf_op jit(solution)/shard_map/all_gather | solution.py:11
  503.7 157.4 %all-gather.41.cloned.1.call-start = ((), (), s32[]{:S(2)}) async-start(), calls=%async_computation.8 | async-start | bytes 2359296 | tf_op jit(solution)/shard_map/all_gather | solution.py:11
  628.9 3.4 copy-start.1
  633.1 175.5 %all-gather.43.cloned.1.call-start = ((), (), s32[]{:S(2)}) async-start(), calls=%async_computation.9 | async-start | bytes 5242880 | tf_op jit(solution)/shard_map/all_gather | solution.py:11
  727.8 137.9 %all-gather.45.cloned.1.call-start = ((), (), s32[]{:S(2)}) async-start(), calls=%async_computation.10 | async-start | bytes 9437184 | tf_op jit(solution)/shard_map/all_gather | solution.py:11
  812.8 108.9 %all-gather.47.cloned.1.call-start = ((), (), s32[]{:S(2)}) async-start(), calls=%async_computation.11 | async-start | bytes 9437184 | tf_op jit(solution)/shard_map/all_gather | solution.py:11
Sparse Core Ops, SparseCore 0:
  13.3 30.4 all-gather.24
  110.0 80.7 all-gather.26
  195.0 52.7 all-gather.28
  250.1 54.2 all-gather.30
  323.5 27.7 all-gather.32
  418.1 80.7 all-gather.34
  503.1 52.7 all-gather.36
  557.7 54.2 all-gather.38
  633.3 27.7 all-gather.40
  727.9 80.7 all-gather.42
  812.9 52.7 all-gather.44
  867.5 54.2 all-gather.46
